TPU v7x, 32 devices: a whole 2x2x4 slice. The times are simulated.
32 devices in a mesh: grp: 2 (over x), area: 8 (over z, y), ctg: 2 (over core).
Axes of the slice: x: 2, y: 2, z: 4, core: 2. Of those that a mesh axis runs over, the one named last changes fastest.
Arguments:
- area_size: int32 [16], P(('grp', 'area')), parts along dimension 0, may hold values from 299 to 1024, as said below
- tie_peer: int32 [16, 42], P(('grp', 'area')), parts along dimension 0, may hold values from 0 to 7, as said below
- kkt_diag: float32 [16, 2, 1024], P(('grp', 'area'), 'ctg'), parts along dimension 0, may hold values from 0.5 to 1
- kkt_offdiag: float32 [16, 2, 1024, 1024], P(('grp', 'area'), 'ctg'), parts along dimension 0, may hold values from -0.1875 to 0.1875
- cost: float32 [16, 2, 1024, 256], P(('grp', 'area'), 'ctg'), parts along dimension 0, may hold values from -6 to 6
- consensus: float32 [16, 2, 1024, 256], P(('grp', 'area'), 'ctg'), parts along dimension 0, may hold values from -4 to 4
- dual: float32 [16, 2, 1024, 256], P(('grp', 'area'), 'ctg'), parts along dimension 0, may hold values from -4 to 4
- limit: float32 [16, 1024, 256], P(('grp', 'area')), parts along dimension 0, may hold values from 0.3 to 1.5
Outputs:
- agreed_out: float32 [16, 2, 1024, 256], P(('grp', 'area'), 'ctg'), parts along dimension 0
- dual_out: float32 [16, 2, 1024, 256], P(('grp', 'area'), 'ctg'), parts along dimension 0
There are 2 independent parts, one for each index of `grp`. A program takes and returns all parts, laid end to end along the dimension named above; each array names one. Nothing has to cross between parts.
Inputs may be any that keep to these rules, and one draw needn't show every extreme that they name: `area_size`: some area has exactly 1024 live slots. `tie_peer`: never the area itself; each area has exactly 6 tie slots to each other area.
All inputs are finite; a program needn't handle non-finite values.
Results may differ from a plain program's by a relative error of at most 0.0003.
Values sent between devices are 32-bit elements; how exact they have to be, the bound alone decides.
No kernel may reach another device: no remote copies, remote signals or barrier semaphores. Data moves between devices by JAX's collectives and lax.ppermute only.
A program may use at most 64 MiB of HBM per device.

v0:
```python
import jax
import jax.numpy as jnp
from jax import lax
from jax.sharding import PartitionSpec as P

GENS = 256
ITERS = 3


def tie_dest(peers, pair_lines):
    count = peers.shape[0]
    order = jnp.arange(count)
    same = (peers[:, None] == peers[None, :]) & (order[:, None] < order[None, :])
    rank = jnp.sum(same.astype(jnp.int32), axis=0)
    return peers * pair_lines + rank


def apply_rows(matrix, right_side):
    return jnp.dot(
        matrix, right_side, precision=lax.Precision.HIGHEST, preferred_element_type=jnp.float32
    )


def local(area_size, tie_peer, kkt_diag, kkt_offdiag, cost, consensus, dual, limit):
    areas = lax.axis_size("area")
    scenarios = lax.axis_size("ctg")
    peers = tie_peer[0]
    ties = peers.shape[0]
    pair_lines = ties // (areas - 1)
    dest = tie_dest(peers, pair_lines)
    slots = cost.shape[2]
    hours = cost.shape[3]
    shared = GENS + ties
    live = (jnp.arange(slots) < area_size[0]).astype(jnp.float32)[:, None]
    offdiag = kkt_offdiag[0, 0]
    diagonal = kkt_diag[0, 0][:, None]
    bound = limit[0]
    linear = cost[0, 0]
    agreed = consensus[0, 0]
    dual_var = dual[0, 0]
    for iteration in range(ITERS):
        right_side = live * (agreed - dual_var - linear)
        primal = live * (diagonal * right_side + apply_rows(offdiag, right_side))
        primal_top = primal[:shared]
        dual_top = dual_var[:shared]
        shifted = primal_top + dual_top
        gen_mean = lax.psum(shifted[:GENS], "ctg") / scenarios
        empty = jnp.zeros((areas * pair_lines, hours), jnp.float32)
        sent_primal = empty.at[dest].set(primal_top[GENS:])
        sent_dual = empty.at[dest].set(dual_top[GENS:])
        got_primal = lax.all_to_all(sent_primal, "area", split_axis=0, concat_axis=0, tiled=True)
        got_dual = lax.all_to_all(sent_dual, "area", split_axis=0, concat_axis=0, tiled=True)
        other = got_primal[dest] + got_dual[dest]
        top_part = jnp.concatenate([gen_mean, 0.5 * (shifted[GENS:] + other)], axis=0)
        averaged = jnp.concatenate([top_part, primal[shared:] + dual_var[shared:]], axis=0)
        agreed = live * jnp.clip(averaged, -bound, bound)
        dual_var = live * (dual_var + primal - agreed)
    return (agreed[None, None], dual_var[None, None])


def solution(mesh):
    return jax.shard_map(
        local,
        mesh=mesh,
        in_specs=(
            P(("grp", "area")),
            P(("grp", "area"), None),
            P(("grp", "area"), "ctg", None),
            P(("grp", "area"), "ctg", None, None),
            P(("grp", "area"), "ctg", None, None),
            P(("grp", "area"), "ctg", None, None),
            P(("grp", "area"), "ctg", None, None),
            P(("grp", "area"), None, None),
        ),
        out_specs=(P(("grp", "area"), "ctg", None, None), P(("grp", "area"), "ctg", None, None)),
        check_vma=False,
    )
```

profile of v0, /device:TPU:0, one launch (start us, length us, event | category | flops | bytes accessed | tf_op | source)
XLA Modules:
  0.0 138.7 jit_solution(8805056950843362891)
XLA Ops:
  7.2 0.8 convert_reduce_fusion
  8.0 0.7 fusion.85
  8.6 1.0 scatter_custom_fusion.1
  9.7 0.6 all_to_all.51
  10.3 7.3 %all-to-all-start.1 = ((f32[8,6,256]{2,1,0:T(8,128)}), f32[8,6,256]{2,1,0:T(8,128)S(1)}, u32[]{:S(2)}, u32[]{:S(2)}) async-start(f32[8,6,256]{2,1,0:T(8,128)} %all_to_all.51), calls=%async_computation.1 | async-start | bytes 131072 | tf_op jit(solution)/shard_map/all_to_all | solution.py:52
  17.6 0.0 all-reduce.4.cloned.1.call-start
  18.3 0.0 copy-start.4
  18.3 7.7 %fusion.12 = f32[1024,256]{1,0:T(8,128)S(1)} fusion(f32[1,1,1024,1024]{3,2,1,0:T(8,128)} %param.11, f32[1,1,1024,256]{3,2,1,0:T(8,128)} %param.12, f32[1,1,1024,256]{3,2,1,0:T(8,128)} %param.14, f32[1,1,1024,256]{3,2,1,0:T(8,128)} %param.13, f32[1024]{0:T(1024)} %bitcast.144, f32[1024]{0:T(1024)S(1)} %fusion.84), kind=kOutput, calls=%fused_computation.20 | convolution fusion | flops 3223584768 | bytes 8396800 | tf_op jit(solution)/shard_map/dot_general | solution.py:19
  26.0 0.0 copy-start.5
  26.0 1.0 copy-done.5
  27.0 0.7 slice.127
  27.8 0.0 all-reduce.4.cloned.1.call-update
  27.8 1.3 slice_add_fusion.2
  29.1 0.0 copy-start.7
  29.1 1.0 scatter_custom_fusion
  30.1 0.6 all_to_all.48
  30.8 6.0 %all-to-all-start = ((f32[8,6,256]{2,1,0:T(8,128)}), f32[8,6,256]{2,1,0:T(8,128)S(1)}, u32[]{:S(2)}, u32[]{:S(2)}) async-start(f32[8,6,256]{2,1,0:T(8,128)} %all_to_all.48), calls=%async_computation | async-start | bytes 131072 | tf_op jit(solution)/shard_map/all_to_all | solution.py:51
  36.7 0.6 gather_fusion.1
  37.4 6.3 %all-to-all-done = f32[8,6,256]{2,1,0:T(8,128)S(1)} async-done(((f32[8,6,256]{2,1,0:T(8,128)}), f32[8,6,256]{2,1,0:T(8,128)S(1)}, u32[]{:S(2)}, u32[]{:S(2)}) %all-to-all-start) | async-done | bytes 49184 | tf_op jit(solution)/shard_map/all_to_all | solution.py:51
  43.6 0.6 gather_fusion
  44.3 3.3 %all-reduce.4.cloned.1.call-done = f32[256,256]{1,0:T(8,128)} async-done(((f32[256,256]{1,0:T(8,128)}), f32[256,256]{1,0:T(8,128)}) %all-reduce.4.cloned.1.call-update) | async-done | bytes 262160 | tf_op jit(solution)/shard_map/psum | solution.py:47
  47.5 1.1 broadcast_multiply_fusion.2
  48.7 2.1 %fusion.50 = f32[1024,256]{1,0:T(8,128)S(1)} fusion(f32[1024,256]{1,0:T(8,128)} %copy-done.5, f32[1,1,1024,256]{3,2,1,0:T(8,128)} %param.14, f32[1024]{0:T(1024)S(1)} %fusion.84, f32[726,256]{1,0:T(8,128)S(1)} %slice_add_fusion.2, f32[42,256]{1,0:T(8,128)S(1)} %fusion.73, f32[256,256]{1,0:T(8,128)S(1)} %broadcast_multiply_fusion.2, ...), kind=kLoop, calls=%fused_computation.53 | loop fusion | flops 2359296 | bytes 5246976 | tf_op jit(solution)/shard_map/mul | solution.py:57
  50.8 6.5 %fusion.21 = f32[1024,256]{1,0:T(8,128)} fusion(f32[1,1,1024,1024]{3,2,1,0:T(8,128)S(1)} %copy-done, f32[1,1,1024,256]{3,2,1,0:T(8,128)} %param.12, f32[1024,256]{1,0:T(8,128)S(1)} %fusion.50, f32[1024]{0:T(1024)S(1)} %bitcast.145, f32[1024]{0:T(1024)S(1)} %fusion.84, f32[726,256]{1,0:T(8,128)S(1)} %slice_add_fusion.2, f32[42,256]{1,0:T(8,128)S(1)} %fusion.73, ...), kind=kOutput, calls=%fused_computation.23 | convolution fusion | flops 3226730496 | bytes 9445376 | tf_op jit(solution)/shard_map/dot_general | solution.py:19
  57.4 1.0 scatter_custom_fusion.2
  58.4 0.6 all_to_all.54
  59.0 5.8 %all-to-all-start.2 = ((f32[8,6,256]{2,1,0:T(8,128)}), f32[8,6,256]{2,1,0:T(8,128)S(1)}, u32[]{:S(2)}, u32[]{:S(2)}) async-start(f32[8,6,256]{2,1,0:T(8,128)} %all_to_all.54), calls=%async_computation.2 | async-start | bytes 131072 | tf_op jit(solution)/shard_map/all_to_all | solution.py:51
  64.8 0.0 all-reduce.6.cloned.1.call-start
  64.9 1.0 slice_add_fusion.4
  65.9 0.7 scatter_custom_fusion.3
  66.6 0.6 all_to_all.57
  67.3 0.7 slice.133
  68.0 0.0 all-reduce.6.cloned.1.call-update
  68.0 3.7 %all-to-all-done.2 = f32[8,6,256]{2,1,0:T(8,128)S(1)} async-done(((f32[8,6,256]{2,1,0:T(8,128)}), f32[8,6,256]{2,1,0:T(8,128)S(1)}, u32[]{:S(2)}, u32[]{:S(2)}) %all-to-all-start.2) | async-done | bytes 49184 | tf_op jit(solution)/shard_map/all_to_all | solution.py:51
  71.8 3.5 %all-to-all-start.3 = ((f32[8,6,256]{2,1,0:T(8,128)}), f32[8,6,256]{2,1,0:T(8,128)S(1)}, u32[]{:S(2)}, u32[]{:S(2)}) async-start(f32[8,6,256]{2,1,0:T(8,128)} %all_to_all.57), calls=%async_computation.3 | async-start | bytes 131072 | tf_op jit(solution)/shard_map/all_to_all | solution.py:52
  75.3 2.1 %slice_add_fusion.1 = f32[726,256]{1,0:T(8,128)} fusion(f32[1024,256]{1,0:T(8,128)S(1)} %fusion.50, f32[1024,256]{1,0:T(8,128)} %fusion.21), kind=kLoop, calls=%fused_computation.63 | loop fusion | flops 185856 | bytes 2230272 | tf_op jit(solution)/shard_map/add | solution.py:55
  77.4 0.6 gather_fusion.2
  78.0 3.9 %all-to-all-done.3 = f32[8,6,256]{2,1,0:T(8,128)S(1)} async-done(((f32[8,6,256]{2,1,0:T(8,128)}), f32[8,6,256]{2,1,0:T(8,128)S(1)}, u32[]{:S(2)}, u32[]{:S(2)}) %all-to-all-start.3) | async-done | bytes 49184 | tf_op jit(solution)/shard_map/all_to_all | solution.py:52
  82.0 0.6 gather_fusion.3
  82.6 5.1 %all-reduce.6.cloned.1.call-done = f32[256,256]{1,0:T(8,128)} async-done(((f32[256,256]{1,0:T(8,128)}), f32[256,256]{1,0:T(8,128)}) %all-reduce.6.cloned.1.call-update) | async-done | bytes 262160 | tf_op jit(solution)/shard_map/psum | solution.py:47
  87.7 1.1 broadcast_multiply_fusion.1
  88.9 2.3 %subtract_multiply_fusion = f32[1024,256]{1,0:T(8,128)S(1)} fusion(f32[1024,256]{1,0:T(8,128)S(1)} %fusion.50, f32[1024,256]{1,0:T(8,128)} %fusion.21, f32[1024]{0:T(1024)S(1)} %fusion.84, f32[726,256]{1,0:T(8,128)} %slice_add_fusion.1, f32[42,256]{1,0:T(8,128)S(1)} %fusion.70, f32[256,256]{1,0:T(8,128)S(1)} %broadcast_multiply_fusion.1, ...), kind=kLoop, calls=%fused_computation.57 | loop fusion | flops 2359296 | bytes 5246976 | tf_op jit(solution)/shard_map/mul | solution.py:57
  91.2 5.6 %fusion.30 = f32[1024,256]{1,0:T(8,128)S(1)} fusion(f32[1,1,1024,1024]{3,2,1,0:T(8,128)S(1)} %copy-done.1, f32[1,1,1024,256]{3,2,1,0:T(8,128)} %param.12, f32[1024,256]{1,0:T(8,128)S(1)} %subtract_multiply_fusion, f32[1024]{0:T(1024)S(1)} %bitcast.146, f32[1024]{0:T(1024)S(1)} %fusion.84, f32[726,256]{1,0:T(8,128)S(1)} %copy-done.3, ...), kind=kOutput, calls=%fused_computation.26 | convolution fusion | flops 3226730496 | bytes 9445376 | tf_op jit(solution)/shard_map/dot_general | solution.py:19
  96.8 0.7 scatter_custom_fusion.4
  97.5 0.6 all_to_all.60
  98.2 5.8 %all-to-all-start.4 = ((f32[8,6,256]{2,1,0:T(8,128)}), f32[8,6,256]{2,1,0:T(8,128)}, u32[]{:S(2)}, u32[]{:S(2)}) async-start(f32[8,6,256]{2,1,0:T(8,128)} %all_to_all.60), calls=%async_computation.4 | async-start | bytes 131072 | tf_op jit(solution)/shard_map/all_to_all | solution.py:51
  104.0 0.0 all-reduce.8.cloned.1.call-start
  104.1 0.7 scatter_custom_fusion.5
  104.8 0.6 all_to_all.63
  105.5 0.7 slice.141
  106.2 0.0 all-reduce.8.cloned.1.call-update
  106.2 4.8 %all-to-all-done.4 = f32[8,6,256]{2,1,0:T(8,128)} async-done(((f32[8,6,256]{2,1,0:T(8,128)}), f32[8,6,256]{2,1,0:T(8,128)}, u32[]{:S(2)}, u32[]{:S(2)}) %all-to-all-start.4) | async-done | bytes 49184 | tf_op jit(solution)/shard_map/all_to_all | solution.py:51
  111.0 4.0 %all-to-all-start.5 = ((f32[8,6,256]{2,1,0:T(8,128)}), f32[8,6,256]{2,1,0:T(8,128)}, u32[]{:S(2)}, u32[]{:S(2)}) async-start(f32[8,6,256]{2,1,0:T(8,128)} %all_to_all.63), calls=%async_computation.5 | async-start | bytes 131072 | tf_op jit(solution)/shard_map/all_to_all | solution.py:52
  115.0 1.0 slice_add_fusion
  116.0 0.8 all_to_all.62
  116.8 1.2 gather_fusion.4
  118.0 3.9 %all-to-all-done.5 = f32[8,6,256]{2,1,0:T(8,128)} async-done(((f32[8,6,256]{2,1,0:T(8,128)}), f32[8,6,256]{2,1,0:T(8,128)}, u32[]{:S(2)}, u32[]{:S(2)}) %all-to-all-start.5) | async-done | bytes 49184 | tf_op jit(solution)/shard_map/all_to_all | solution.py:52
  121.9 0.8 all_to_all.65
  122.7 1.2 gather_fusion.5
  124.0 0.8 fusion.65
  124.8 2.5 %all-reduce.8.cloned.1.call-done = f32[256,256]{1,0:T(8,128)} async-done(((f32[256,256]{1,0:T(8,128)}), f32[256,256]{1,0:T(8,128)}) %all-reduce.8.cloned.1.call-update) | async-done | bytes 262160 | tf_op jit(solution)/shard_map/psum | solution.py:47
  127.3 1.1 broadcast_multiply_fusion
  128.4 2.5 %fusion.43 = f32[1,1,1024,256]{3,2,1,0:T(8,128)} fusion(f32[726,256]{1,0:T(8,128)} %slice_add_fusion, f32[42,256]{1,0:T(8,128)S(1)} %fusion.65, f32[256,256]{1,0:T(8,128)S(1)} %get-tuple-element.8, f32[1,1024,256]{2,1,0:T(8,128)S(1)} %copy-done.2, f32[1024,256]{1,0:T(8,128)S(1)} %subtract_multiply_fusion, f32[1024,256]{1,0:T(8,128)S(1)} %fusion.30, ...), kind=kLoop, calls=%fused_computation.41 | loop fusion | flops 2359296 | bytes 5246976 | tf_op jit(solution)/shard_map/broadcast_in_dim | solution.py:58
  130.9 1.3 fusion.38
  (23 shorter events, 0.2 us)
Async XLA Ops:
  10.3 20.5 %all-to-all-start.1 = ((f32[8,6,256]{2,1,0:T(8,128)}), f32[8,6,256]{2,1,0:T(8,128)S(1)}, u32[]{:S(2)}, u32[]{:S(2)}) async-start(f32[8,6,256]{2,1,0:T(8,128)} %all_to_all.51), calls=%async_computation.1 | async-start | bytes 131072 | tf_op jit(solution)/shard_map/all_to_all | solution.py:52
  17.6 29.9 %all-reduce.4.cloned.1.call-start = ((), (), s32[]{:S(2)}) async-start(), calls=%async_computation.6 | async-start | bytes 524288 | tf_op jit(solution)/shard_map/psum | solution.py:47
  18.3 8.7 %copy-start.4 = (f32[1,1,1024,256]{3,2,1,0:T(8,128)S(1)}, f32[1,1,1024,256]{3,2,1,0:T(8,128)}, u32[]{:S(2)}) copy-start(f32[1,1,1024,256]{3,2,1,0:T(8,128)} %param.14) | copy-start | bytes 3145732
  26.0 1.0 copy-start.5
  27.0 21.7 %copy-start.2 = (f32[1,1024,256]{2,1,0:T(8,128)S(1)}, f32[1,1024,256]{2,1,0:T(8,128)}, u32[]{:S(2)}) copy-start(f32[1,1024,256]{2,1,0:T(8,128)} %param.15) | copy-start | bytes 3145732
  29.1 21.7 %copy-start.7 = (f32[1,1,1024]{2,1,0:T(1,128)S(1)}, f32[1,1,1024]{2,1,0:T(1,128)}, u32[]{:S(2)}) copy-start(f32[1,1,1024]{2,1,0:T(1,128)} %param.10) | copy-start | bytes 12292
  30.8 12.9 %all-to-all-start = ((f32[8,6,256]{2,1,0:T(8,128)}), f32[8,6,256]{2,1,0:T(8,128)S(1)}, u32[]{:S(2)}, u32[]{:S(2)}) async-start(f32[8,6,256]{2,1,0:T(8,128)} %all_to_all.48), calls=%async_computation | async-start | bytes 131072 | tf_op jit(solution)/shard_map/all_to_all | solution.py:51
  47.5 3.3 %copy-start = (f32[1,1,1024,1024]{3,2,1,0:T(8,128)S(1)}, f32[1,1,1024,1024]{3,2,1,0:T(8,128)}, u32[]{:S(2)}) copy-start(f32[1,1,1024,1024]{3,2,1,0:T(8,128)} %param.11) | copy-start | bytes 12582916
  59.0 12.7 %all-to-all-start.2 = ((f32[8,6,256]{2,1,0:T(8,128)}), f32[8,6,256]{2,1,0:T(8,128)S(1)}, u32[]{:S(2)}, u32[]{:S(2)}) async-start(f32[8,6,256]{2,1,0:T(8,128)} %all_to_all.54), calls=%async_computation.2 | async-start | bytes 131072 | tf_op jit(solution)/shard_map/all_to_all | solution.py:51
  64.8 22.9 %all-reduce.6.cloned.1.call-start = ((), (), s32[]{:S(2)}) async-start(), calls=%async_computation.7 | async-start | bytes 524288 | tf_op jit(solution)/shard_map/psum | solution.py:47
  71.8 10.2 %all-to-all-start.3 = ((f32[8,6,256]{2,1,0:T(8,128)}), f32[8,6,256]{2,1,0:T(8,128)S(1)}, u32[]{:S(2)}, u32[]{:S(2)}) async-start(f32[8,6,256]{2,1,0:T(8,128)} %all_to_all.57), calls=%async_computation.3 | async-start | bytes 131072 | tf_op jit(solution)/shard_map/all_to_all | solution.py:52
  87.7 3.4 %copy-start.1 = (f32[1,1,1024,1024]{3,2,1,0:T(8,128)S(1)}, f32[1,1,1024,1024]{3,2,1,0:T(8,128)}, u32[]{:S(2)}) copy-start(f32[1,1,1024,1024]{3,2,1,0:T(8,128)} %param.11) | copy-start | bytes 12582916
  87.7 3.4 %copy-start.3 = (f32[726,256]{1,0:T(8,128)S(1)}, f32[726,256]{1,0:T(8,128)}, u32[]{:S(2)}) copy-start(f32[726,256]{1,0:T(8,128)} %slice_add_fusion.1) | copy-start | bytes 2230276
  98.2 12.8 %all-to-all-start.4 = ((f32[8,6,256]{2,1,0:T(8,128)}), f32[8,6,256]{2,1,0:T(8,128)}, u32[]{:S(2)}, u32[]{:S(2)}) async-start(f32[8,6,256]{2,1,0:T(8,128)} %all_to_all.60), calls=%async_computation.4 | async-start | bytes 131072 | tf_op jit(solution)/shard_map/all_to_all | solution.py:51
  104.0 23.3 %all-reduce.8.cloned.1.call-start = ((), (), s32[]{:S(2)}) async-start(), calls=%async_computation.8 | async-start | bytes 524288 | tf_op jit(solution)/shard_map/psum | solution.py:47
  111.0 10.9 %all-to-all-start.5 = ((f32[8,6,256]{2,1,0:T(8,128)}), f32[8,6,256]{2,1,0:T(8,128)}, u32[]{:S(2)}, u32[]{:S(2)}) async-start(f32[8,6,256]{2,1,0:T(8,128)} %all_to_all.63), calls=%async_computation.5 | async-start | bytes 131072 | tf_op jit(solution)/shard_map/all_to_all | solution.py:52
  127.3 3.5 %copy-start.6 = (f32[726,256]{1,0:T(8,128)S(1)}, f32[726,256]{1,0:T(8,128)}, u32[]{:S(2)}) copy-start(f32[726,256]{1,0:T(8,128)} %slice_add_fusion) | copy-start | bytes 2230276
Sparse Core Ops, SparseCore 0:
  27.9 19.5 all-reduce.3
  68.1 19.5 all-reduce.5
  107.7 19.5 all-reduce.7
where the time goes:
time: 140 us; the launch traced here: 139 us
  waiting for transfers between devices  33.6 us (24%)
  starting transfers between devices  32.5 us (23%)
  matrix products  19.9 us (14%)
  other arithmetic  19.3 us (14%)
  local copies, waits for them, and re-layouts  18.8 us (13%)
  between operations  14.6 us (10%)
    dot_general x3, matrix products, apply_rows(): jnp.dot(matrix, right_side, precision=lax.Precision.HIGHEST, preferred_el...  19.9 us
    all_to_all x3, starting transfers between devices, local(): lax.all_to_all(sent_primal, 'area', split_axis=0, concat_axis=0, tiled=True)  17.6 us
    all_to_all x3, starting transfers between devices, local(): lax.all_to_all(sent_dual, 'area', split_axis=0, concat_axis=0, tiled=True)  14.8 us
    all_to_all x3, waiting for transfers between devices, local(): lax.all_to_all(sent_primal, 'area', split_axis=0, concat_axis=0, tiled=True)  14.8 us
    psum x3, waiting for transfers between devices, local(): gen_mean = lax.psum(shifted[:GENS], 'ctg') / scenarios  10.9 us
    all_to_all x3, waiting for transfers between devices, local(): lax.all_to_all(sent_dual, 'area', split_axis=0, concat_axis=0, tiled=True)  7.78 us
    gather x6, local copies, waits for them, and re-layouts, local(): other = got_primal[dest] + got_dual[dest]  4.91 us
    mul x2, other arithmetic, local(): dual_var = live * (dual_var + primal - agreed)  4.41 us
  transfers between devices with their start and end apart: 9, of which 8 were waited for; matrix products, arithmetic and copies ran while one was open for 17% of the time, Pallas kernels for 0%

commit v1 on v0

--- a/solution.py
+++ b/solution.py
@@ -1,3 +1,4 @@
+import functools
 import jax
 import jax.numpy as jnp
 from jax import lax
@@ -5,6 +6,14 @@
 
 GENS = 256
 ITERS = 3
+
+
+def _lay_series_all(field_in, peer_axis):
+    piece_next = lax.all_gather(field_in, peer_axis).sum(axis=0)
+    return piece_next
+
+
+place_weights = functools.partial(_lay_series_all, peer_axis="ctg")
 
 
 def tie_dest(peers, pair_lines):
@@ -44,7 +53,7 @@
         primal_top = primal[:shared]
         dual_top = dual_var[:shared]
         shifted = primal_top + dual_top
-        gen_mean = lax.psum(shifted[:GENS], "ctg") / scenarios
+        gen_mean = place_weights(shifted[:GENS]) / scenarios
         empty = jnp.zeros((areas * pair_lines, hours), jnp.float32)
         sent_primal = empty.at[dest].set(primal_top[GENS:])
         sent_dual = empty.at[dest].set(dual_top[GENS:])

time: 140 us -> 117 us (0.84)
  waiting for transfers between devices: 33.6 us -> 19.8 us
  between operations: 14.6 us -> 1.59 us
  blocking collectives: 0 us -> 6.68 us
  starting transfers between devices: 32.5 us -> 28.1 us
  other arithmetic: 19.3 us -> 22.9 us
    psum x3 -> x0, waiting for transfers between devices: 10.9 us -> none  [local(): gen_mean = lax.psum(shifted[:GENS], 'ctg') / scenarios]
    all_gather x0 -> x3, blocking collectives: none -> 6.68 us  [_lay_series_all(): piece_next = lax.all_gather(field_in, peer_axis).sum(axis=0)]
    all_to_all x3, starting transfers between devices: 17.6 us -> 13.3 us  [local(): lax.all_to_all(sent_primal, 'area', split_axis=0, concat_axis=0, tiled=True)]
    reduce_sum x0 -> x3, other arithmetic: none -> 3.25 us  [_lay_series_all(): piece_next = lax.all_gather(field_in, peer_axis).sum(axis=0)]
    all_to_all x3, waiting for transfers between devices: 14.8 us -> 11.7 us  [local(): lax.all_to_all(sent_primal, 'area', split_axis=0, concat_axis=0, tiled=True)]
    slice x3, local copies, waits for them, and re-layouts: 2.15 us -> 0.05 us  [local(): gen_mean = place_weights(shifted[:GENS]) / scenarios]
  transfers between devices with their start and end apart: 9 -> 6, of which waited for: 8 -> 5; matrix products, arithmetic and copies ran while one was open for 17% -> 16% of each run, Pallas kernels for 0% -> 0%
where the time goes in v1:
time: 117 us; the launch traced here: 116 us
  starting transfers between devices  28.1 us (24%)
  other arithmetic  22.9 us (20%)
  waiting for transfers between devices  19.8 us (17%)
  matrix products  18.6 us (16%)
  local copies, waits for them, and re-layouts  18.1 us (15%)
  blocking collectives  6.68 us (6%)
  between operations  1.59 us (1%)
    dot_general x3, matrix products, apply_rows(): jnp.dot(matrix, right_side, precision=lax.Precision.HIGHEST, preferred_el...  18.6 us
    all_to_all x3, starting transfers between devices, local(): lax.all_to_all(sent_dual, 'area', split_axis=0, concat_axis=0, tiled=True)  14.8 us
    all_to_all x3, starting transfers between devices, local(): lax.all_to_all(sent_primal, 'area', split_axis=0, concat_axis=0, tiled=True)  13.3 us
    all_to_all x3, waiting for transfers between devices, local(): lax.all_to_all(sent_primal, 'area', split_axis=0, concat_axis=0, tiled=True)  11.7 us
    all_to_all x3, waiting for transfers between devices, local(): lax.all_to_all(sent_dual, 'area', split_axis=0, concat_axis=0, tiled=True)  8.12 us
    all_gather x3, blocking collectives, _lay_series_all(): piece_next = lax.all_gather(field_in, peer_axis).sum(axis=0)  6.68 us
    gather x6, local copies, waits for them, and re-layouts, local(): other = got_primal[dest] + got_dual[dest]  4.92 us
    mul x2, other arithmetic, local(): dual_var = live * (dual_var + primal - agreed)  4.38 us
  transfers between devices with their start and end apart: 6, of which 5 were waited for; matrix products, arithmetic and copies ran while one was open for 16% of the time, Pallas kernels for 0%

profile of v1, /device:TPU:0, one launch (start us, length us, event | category | flops | bytes accessed | tf_op | source)
XLA Modules:
  0.0 115.8 jit_solution(7200170239035523543)
XLA Ops:
  0.6 0.8 convert_reduce_fusion
  1.5 0.7 fusion.85
  2.1 1.0 scatter_custom_fusion.1
  3.1 0.6 all_to_all.51
  3.7 7.3 %all-to-all-start.1 = ((f32[8,6,256]{2,1,0:T(8,128)}), f32[8,6,256]{2,1,0:T(8,128)S(1)}, u32[]{:S(2)}, u32[]{:S(2)}) async-start(f32[8,6,256]{2,1,0:T(8,128)} %all_to_all.51), calls=%async_computation.1 | async-start | bytes 131072 | tf_op jit(solution)/shard_map/all_to_all | solution.py:61
  11.7 0.0 copy-start.3
  11.7 7.7 %fusion.12 = f32[1024,256]{1,0:T(8,128)S(1)} fusion(f32[1,1,1024,1024]{3,2,1,0:T(8,128)} %param.11, f32[1,1,1024,256]{3,2,1,0:T(8,128)} %param.12, f32[1,1,1024,256]{3,2,1,0:T(8,128)} %param.14, f32[1,1,1024,256]{3,2,1,0:T(8,128)} %param.13, f32[1024]{0:T(1024)} %bitcast.150, f32[1024]{0:T(1024)S(1)} %fusion.84), kind=kOutput, calls=%fused_computation.20 | convolution fusion | flops 3223584768 | bytes 8396800 | tf_op jit(solution)/shard_map/dot_general | solution.py:28
  19.5 0.0 copy-start.4
  19.5 0.0 copy-start.2
  19.6 0.0 copy-start.7
  19.6 0.2 slice_add_fusion.2
  19.7 0.6 copy-done.7
  20.3 2.2 %all-gather = f32[512,256]{1,0:T(8,128)S(1)} all-gather(f32[256,256]{1,0:T(8,128)S(1)} %slice.127), channel_id=2, replica_groups=mesh['grp'=2,'area'=8,'ctg'=2] {'ctg'}, dimensions={0}, use_global_device_ids=true | all-gather | bytes 786432 | tf_op jit(solution)/shard_map/all_gather | solution.py:12
  22.5 0.7 reduce_sum.38
  23.2 1.0 broadcast_multiply_fusion.2
  24.2 0.7 scatter_custom_fusion
  24.9 0.6 all_to_all.48
  25.6 6.0 %all-to-all-start = ((f32[8,6,256]{2,1,0:T(8,128)}), f32[8,6,256]{2,1,0:T(8,128)S(1)}, u32[]{:S(2)}, u32[]{:S(2)}) async-start(f32[8,6,256]{2,1,0:T(8,128)} %all_to_all.48), calls=%async_computation | async-start | bytes 131072 | tf_op jit(solution)/shard_map/all_to_all | solution.py:60
  31.6 0.6 gather_fusion.1
  32.2 6.3 %all-to-all-done = f32[8,6,256]{2,1,0:T(8,128)S(1)} async-done(((f32[8,6,256]{2,1,0:T(8,128)}), f32[8,6,256]{2,1,0:T(8,128)S(1)}, u32[]{:S(2)}, u32[]{:S(2)}) %all-to-all-start) | async-done | bytes 49184 | tf_op jit(solution)/shard_map/all_to_all | solution.py:60
  38.5 0.6 gather_fusion
  39.1 0.0 copy-start
  39.1 0.0 copy-start.5
  39.1 1.0 fusion.73
  40.1 2.4 %fusion.50 = f32[1024,256]{1,0:T(8,128)S(1)} fusion(f32[1024,256]{1,0:T(8,128)} %copy-done.4, f32[1,1,1024,256]{3,2,1,0:T(8,128)} %param.14, f32[1024]{0:T(1024)S(1)} %fusion.84, f32[726,256]{1,0:T(8,128)S(1)} %slice_add_fusion.2, f32[42,256]{1,0:T(8,128)S(1)} %fusion.73, f32[256,256]{1,0:T(8,128)S(1)} %broadcast_multiply_fusion.2, ...), kind=kLoop, calls=%fused_computation.53 | loop fusion | flops 2359296 | bytes 5246976 | tf_op jit(solution)/shard_map/mul | solution.py:66
  42.6 4.9 %fusion.21 = f32[1024,256]{1,0:T(8,128)} fusion(f32[1,1,1024,1024]{3,2,1,0:T(8,128)S(1)} %copy-done, f32[1,1,1024,256]{3,2,1,0:T(8,128)S(1)} %copy-done.5, f32[1024,256]{1,0:T(8,128)S(1)} %fusion.50, f32[1024]{0:T(1024)S(1)} %bitcast.151, f32[1024]{0:T(1024)S(1)} %fusion.84, f32[726,256]{1,0:T(8,128)S(1)} %slice_add_fusion.2, f32[42,256]{1,0:T(8,128)S(1)} %fusion.73, ...), kind=kOutput, calls=%fused_computation.23 | convolution fusion | flops 3226730496 | bytes 9445376 | tf_op jit(solution)/shard_map/dot_general | solution.py:28
  47.5 0.7 scatter_custom_fusion.3
  48.2 1.0 scatter_custom_fusion.2
  49.3 1.0 slice_add_fusion.4
  50.3 2.1 %slice_add_fusion.1 = f32[726,256]{1,0:T(8,128)} fusion(f32[1024,256]{1,0:T(8,128)S(1)} %fusion.50, f32[1024,256]{1,0:T(8,128)} %fusion.21), kind=kLoop, calls=%fused_computation.63 | loop fusion | flops 185856 | bytes 2230272 | tf_op jit(solution)/shard_map/add | solution.py:64
  52.4 0.6 all_to_all.54
  53.0 3.3 %all-to-all-start.2 = ((f32[8,6,256]{2,1,0:T(8,128)}), f32[8,6,256]{2,1,0:T(8,128)S(1)}, u32[]{:S(2)}, u32[]{:S(2)}) async-start(f32[8,6,256]{2,1,0:T(8,128)} %all_to_all.54), calls=%async_computation.2 | async-start | bytes 131072 | tf_op jit(solution)/shard_map/all_to_all | solution.py:60
  56.4 0.6 all_to_all.57
  57.0 2.2 %all-gather.1 = f32[512,256]{1,0:T(8,128)S(1)} all-gather(f32[256,256]{1,0:T(8,128)S(1)} %slice.133), channel_id=3, replica_groups=mesh['grp'=2,'area'=8,'ctg'=2] {'ctg'}, dimensions={0}, use_global_device_ids=true | all-gather | bytes 786432 | tf_op jit(solution)/shard_map/all_gather | solution.py:12
  59.2 0.7 reduce_sum.41
  59.9 3.3 %all-to-all-done.2 = f32[8,6,256]{2,1,0:T(8,128)S(1)} async-done(((f32[8,6,256]{2,1,0:T(8,128)}), f32[8,6,256]{2,1,0:T(8,128)S(1)}, u32[]{:S(2)}, u32[]{:S(2)}) %all-to-all-start.2) | async-done | bytes 49184 | tf_op jit(solution)/shard_map/all_to_all | solution.py:60
  63.2 3.5 %all-to-all-start.3 = ((f32[8,6,256]{2,1,0:T(8,128)}), f32[8,6,256]{2,1,0:T(8,128)S(1)}, u32[]{:S(2)}, u32[]{:S(2)}) async-start(f32[8,6,256]{2,1,0:T(8,128)} %all_to_all.57), calls=%async_computation.3 | async-start | bytes 131072 | tf_op jit(solution)/shard_map/all_to_all | solution.py:61
  66.8 1.0 broadcast_multiply_fusion.1
  67.7 0.6 gather_fusion.2
  68.4 5.1 %all-to-all-done.3 = f32[8,6,256]{2,1,0:T(8,128)S(1)} async-done(((f32[8,6,256]{2,1,0:T(8,128)}), f32[8,6,256]{2,1,0:T(8,128)S(1)}, u32[]{:S(2)}, u32[]{:S(2)}) %all-to-all-start.3) | async-done | bytes 49184 | tf_op jit(solution)/shard_map/all_to_all | solution.py:61
  73.4 0.6 gather_fusion.3
  74.0 0.0 copy-start.1
  74.1 2.0 %subtract_multiply_fusion = f32[1024,256]{1,0:T(8,128)S(1)} fusion(f32[1024,256]{1,0:T(8,128)S(1)} %fusion.50, f32[1024,256]{1,0:T(8,128)} %fusion.21, f32[1024]{0:T(1024)S(1)} %fusion.84, f32[726,256]{1,0:T(8,128)} %slice_add_fusion.1, f32[42,256]{1,0:T(8,128)S(1)} %fusion.70, f32[256,256]{1,0:T(8,128)S(1)} %broadcast_multiply_fusion.1, ...), kind=kLoop, calls=%fused_computation.57 | loop fusion | flops 2359296 | bytes 5246976 | tf_op jit(solution)/shard_map/mul | solution.py:66
  76.1 0.7 copy-done.1
  76.8 5.9 %fusion.30 = f32[1024,256]{1,0:T(8,128)S(1)} fusion(f32[1,1,1024,1024]{3,2,1,0:T(8,128)S(1)} %copy-done.1, f32[1,1,1024,256]{3,2,1,0:T(8,128)} %param.12, f32[1024,256]{1,0:T(8,128)S(1)} %subtract_multiply_fusion, f32[1024]{0:T(1024)S(1)} %bitcast.152, f32[1024]{0:T(1024)S(1)} %fusion.84, f32[726,256]{1,0:T(8,128)} %slice_add_fusion.1, ...), kind=kOutput, calls=%fused_computation.26 | convolution fusion | flops 3226730496 | bytes 9445376 | tf_op jit(solution)/shard_map/dot_general | solution.py:28
  82.7 0.7 scatter_custom_fusion.5
  83.5 1.3 %scatter_custom_fusion.4 = f32[48,256]{1,0:T(8,128)} fusion(s32[42]{0:T(128)S(1)} %fusion.85, f32[1024,256]{1,0:T(8,128)S(1)} %fusion.30, f32[]{:T(128)} %constant.5.clone.1), kind=kCustom, calls=%fused_computation.76 | custom fusion | bytes 98308 | tf_op jit(solution)/shard_map/scatter | solution.py:58
  84.8 1.0 slice_add_fusion
  85.8 1.4 %all_to_all.60 = f32[8,6,256]{2,1,0:T(8,128)} reshape(f32[48,256]{1,0:T(8,128)} %scatter_custom_fusion.4) | data formatting | bytes 98304 | tf_op jit(solution)/shard_map/all_to_all | solution.py:60
  87.2 4.0 %all-to-all-start.4 = ((f32[8,6,256]{2,1,0:T(8,128)}), f32[8,6,256]{2,1,0:T(8,128)}, u32[]{:S(2)}, u32[]{:S(2)}) async-start(f32[8,6,256]{2,1,0:T(8,128)} %all_to_all.60), calls=%async_computation.4 | async-start | bytes 131072 | tf_op jit(solution)/shard_map/all_to_all | solution.py:60
  91.2 0.6 all_to_all.63
  91.9 2.3 %all-gather.2 = f32[512,256]{1,0:T(8,128)} all-gather(f32[256,256]{1,0:T(8,128)S(1)} %slice.141), channel_id=4, replica_groups=mesh['grp'=2,'area'=8,'ctg'=2] {'ctg'}, dimensions={0}, use_global_device_ids=true | all-gather | bytes 786432 | tf_op jit(solution)/shard_map/all_gather | solution.py:12
  94.2 1.8 %reduce_sum.42 = f32[256,256]{1,0:T(8,128)} reduce(f32[2,256,256]{2,1,0:T(8,128)} %bitcast.146, f32[]{:T(128)} %constant.5.clone.1), dimensions={0}, to_apply=%region_7.8 | reduce | flops 65536 | bytes 786436 | tf_op jit(solution)/shard_map/reduce_sum | solution.py:12
  96.0 2.2 %all-to-all-done.4 = f32[8,6,256]{2,1,0:T(8,128)} async-done(((f32[8,6,256]{2,1,0:T(8,128)}), f32[8,6,256]{2,1,0:T(8,128)}, u32[]{:S(2)}, u32[]{:S(2)}) %all-to-all-start.4) | async-done | bytes 49184 | tf_op jit(solution)/shard_map/all_to_all | solution.py:60
  98.1 4.0 %all-to-all-start.5 = ((f32[8,6,256]{2,1,0:T(8,128)}), f32[8,6,256]{2,1,0:T(8,128)}, u32[]{:S(2)}, u32[]{:S(2)}) async-start(f32[8,6,256]{2,1,0:T(8,128)} %all_to_all.63), calls=%async_computation.5 | async-start | bytes 131072 | tf_op jit(solution)/shard_map/all_to_all | solution.py:61
  102.1 1.8 %broadcast_multiply_fusion = (f32[256,256]{1,0:T(8,128)}, f32[1,1,256,256]{3,2,1,0:T(8,128)}) fusion(f32[256,256]{1,0:T(8,128)} %reduce_sum.42), kind=kLoop, calls=%fused_computation.71 | loop fusion | flops 65536 | bytes 786432 | tf_op jit(solution)/shard_map/div | solution.py:56
  103.9 0.8 all_to_all.62
  104.7 1.2 %gather_fusion.4 = f32[42,256]{1,0:T(8,128)} fusion(f32[48,256]{1,0:T(8,128)S(1)} %all_to_all.62, s32[1024]{0:T(1024)S(1)} %pad_clamp_fusion), kind=kCustom, calls=%fused_computation.4 | custom fusion | bytes 86184 | tf_op jit(solution)/shard_map/gather | solution.py:62
  106.0 3.1 %all-to-all-done.5 = f32[8,6,256]{2,1,0:T(8,128)} async-done(((f32[8,6,256]{2,1,0:T(8,128)}), f32[8,6,256]{2,1,0:T(8,128)}, u32[]{:S(2)}, u32[]{:S(2)}) %all-to-all-start.5) | async-done | bytes 49184 | tf_op jit(solution)/shard_map/all_to_all | solution.py:61
  109.0 0.8 all_to_all.65
  109.9 1.2 %gather_fusion.5 = f32[42,256]{1,0:T(8,128)} fusion(f32[48,256]{1,0:T(8,128)S(1)} %all_to_all.65, s32[1024]{0:T(1024)S(1)} %pad_clamp_fusion), kind=kCustom, calls=%fused_computation.5 | custom fusion | bytes 86184 | tf_op jit(solution)/shard_map/gather | solution.py:62
  111.1 0.9 fusion.65
  112.0 2.5 %fusion.43 = f32[1,1,1024,256]{3,2,1,0:T(8,128)} fusion(f32[726,256]{1,0:T(8,128)} %slice_add_fusion, f32[42,256]{1,0:T(8,128)S(1)} %fusion.65, f32[256,256]{1,0:T(8,128)} %get-tuple-element.8, f32[1,1024,256]{2,1,0:T(8,128)S(1)} %copy-done.2, f32[1024,256]{1,0:T(8,128)S(1)} %subtract_multiply_fusion, f32[1024,256]{1,0:T(8,128)S(1)} %fusion.30, ...), kind=kLoop, calls=%fused_computation.41 | loop fusion | flops 2359296 | bytes 5246976 | tf_op jit(solution)/shard_map/broadcast_in_dim | solution.py:67
  114.5 1.3 %fusion.38 = f32[1,1,1024,256]{3,2,1,0:T(8,128)} fusion(f32[1,1,726,256]{3,2,1,0:T(8,128)S(1)} %bitcast.145, f32[1,1,42,256]{3,2,1,0:T(8,128)S(1)} %bitcast.149, f32[1,1,256,256]{3,2,1,0:T(8,128)S(1)} %copy-done.8, f32[1,1024,256]{2,1,0:T(8,128)S(1)} %copy-done.2, f32[1024]{0:T(1024)S(1)} %fusion.84), kind=kLoop, calls=%fused_computation.35 | loop fusion | flops 1572864 | bytes 3149824 | tf_op jit(solution)/shard_map/mul | solution.py:65
  (24 shorter events, 0.2 us)
Async XLA Ops:
  3.7 21.8 %all-to-all-start.1 = ((f32[8,6,256]{2,1,0:T(8,128)}), f32[8,6,256]{2,1,0:T(8,128)S(1)}, u32[]{:S(2)}, u32[]{:S(2)}) async-start(f32[8,6,256]{2,1,0:T(8,128)} %all_to_all.51), calls=%async_computation.1 | async-start | bytes 131072 | tf_op jit(solution)/shard_map/all_to_all | solution.py:61
  11.7 7.8 %copy-start.3 = (f32[1,1,1024,256]{3,2,1,0:T(8,128)S(1)}, f32[1,1,1024,256]{3,2,1,0:T(8,128)}, u32[]{:S(2)}) copy-start(f32[1,1,1024,256]{3,2,1,0:T(8,128)} %param.14) | copy-start | bytes 3145732
  19.5 19.6 %copy-start.4 = (f32[1024,256]{1,0:T(8,128)}, f32[1024,256]{1,0:T(8,128)S(1)}, u32[]{:S(2)}) copy-start(f32[1024,256]{1,0:T(8,128)S(1)} %fusion.12) | copy-start | bytes 3145732
  19.5 20.6 %copy-start.2 = (f32[1,1024,256]{2,1,0:T(8,128)S(1)}, f32[1,1024,256]{2,1,0:T(8,128)}, u32[]{:S(2)}) copy-start(f32[1,1024,256]{2,1,0:T(8,128)} %param.15) | copy-start | bytes 3145732
  19.6 0.7 copy-start.7
  22.5 20.0 %copy-start.9 = (f32[1,1,1024]{2,1,0:T(1,128)S(1)}, f32[1,1,1024]{2,1,0:T(1,128)}, u32[]{:S(2)}) copy-start(f32[1,1,1024]{2,1,0:T(1,128)} %param.10) | copy-start | bytes 12292
  25.6 12.9 %all-to-all-start = ((f32[8,6,256]{2,1,0:T(8,128)}), f32[8,6,256]{2,1,0:T(8,128)S(1)}, u32[]{:S(2)}, u32[]{:S(2)}) async-start(f32[8,6,256]{2,1,0:T(8,128)} %all_to_all.48), calls=%async_computation | async-start | bytes 131072 | tf_op jit(solution)/shard_map/all_to_all | solution.py:60
  39.1 3.4 %copy-start = (f32[1,1,1024,1024]{3,2,1,0:T(8,128)S(1)}, f32[1,1,1024,1024]{3,2,1,0:T(8,128)}, u32[]{:S(2)}) copy-start(f32[1,1,1024,1024]{3,2,1,0:T(8,128)} %param.11) | copy-start | bytes 12582916
  39.1 3.4 %copy-start.5 = (f32[1,1,1024,256]{3,2,1,0:T(8,128)S(1)}, f32[1,1,1024,256]{3,2,1,0:T(8,128)}, u32[]{:S(2)}) copy-start(f32[1,1,1024,256]{3,2,1,0:T(8,128)} %param.12) | copy-start | bytes 3145732
  53.0 10.2 %all-to-all-start.2 = ((f32[8,6,256]{2,1,0:T(8,128)}), f32[8,6,256]{2,1,0:T(8,128)S(1)}, u32[]{:S(2)}, u32[]{:S(2)}) async-start(f32[8,6,256]{2,1,0:T(8,128)} %all_to_all.54), calls=%async_computation.2 | async-start | bytes 131072 | tf_op jit(solution)/shard_map/all_to_all | solution.py:60
  63.2 10.2 %all-to-all-start.3 = ((f32[8,6,256]{2,1,0:T(8,128)}), f32[8,6,256]{2,1,0:T(8,128)S(1)}, u32[]{:S(2)}, u32[]{:S(2)}) async-start(f32[8,6,256]{2,1,0:T(8,128)} %all_to_all.57), calls=%async_computation.3 | async-start | bytes 131072 | tf_op jit(solution)/shard_map/all_to_all | solution.py:61
  74.0 2.7 %copy-start.1 = (f32[1,1,1024,1024]{3,2,1,0:T(8,128)S(1)}, f32[1,1,1024,1024]{3,2,1,0:T(8,128)}, u32[]{:S(2)}) copy-start(f32[1,1,1024,1024]{3,2,1,0:T(8,128)} %param.11) | copy-start | bytes 12582916
  87.2 10.9 %all-to-all-start.4 = ((f32[8,6,256]{2,1,0:T(8,128)}), f32[8,6,256]{2,1,0:T(8,128)}, u32[]{:S(2)}, u32[]{:S(2)}) async-start(f32[8,6,256]{2,1,0:T(8,128)} %all_to_all.60), calls=%async_computation.4 | async-start | bytes 131072 | tf_op jit(solution)/shard_map/all_to_all | solution.py:60
  98.1 10.9 %all-to-all-start.5 = ((f32[8,6,256]{2,1,0:T(8,128)}), f32[8,6,256]{2,1,0:T(8,128)}, u32[]{:S(2)}, u32[]{:S(2)}) async-start(f32[8,6,256]{2,1,0:T(8,128)} %all_to_all.63), calls=%async_computation.5 | async-start | bytes 131072 | tf_op jit(solution)/shard_map/all_to_all | solution.py:61
  111.1 3.5 %copy-start.6 = (f32[726,256]{1,0:T(8,128)S(1)}, f32[726,256]{1,0:T(8,128)}, u32[]{:S(2)}) copy-start(f32[726,256]{1,0:T(8,128)} %slice_add_fusion) | copy-start | bytes 2230276
  111.1 3.5 %copy-start.8 = (f32[1,1,256,256]{3,2,1,0:T(8,128)S(1)}, f32[1,1,256,256]{3,2,1,0:T(8,128)}, u32[]{:S(2)}) copy-start(f32[1,1,256,256]{3,2,1,0:T(8,128)} %get-tuple-element.9) | copy-start | bytes 786436
